TPU v7x, 512 devices: a whole 4x8x8 slice. The times are simulated.
512 devices in a mesh: group: 8 (over z), ray: 64 (over y, x, core).
Axes of the slice: x: 4, y: 8, z: 8, core: 2. Of those that a mesh axis runs over, the one named last changes fastest.
Arguments:
- bricks: bfloat16 [16384, 4096], P(('group', 'ray')), may hold values from -6 to 6
- work_bricks: int32 [8, 128], P('group', 'ray'), may hold values from 0 to 16383, as said below
- interp: bfloat16 [32768, 5, 512], P(('group', 'ray')), may hold values from 0 to 0.25
- tile_slot: int32 [32768, 5], P(('group', 'ray')), may hold values from 0 to 127, as said below
- spacing: float32 [32768, 40], P(('group', 'ray')), may hold values from 0.02 to 0.3
- targets: float32 [3, 32768], P(None, ('group', 'ray')), may hold values from 0 to 1
- weight_in: bfloat16 [64, 256], replicated, may hold values from -0.75 to 0.75
- weight_mid: bfloat16 [256, 256], replicated, may hold values from -0.375 to 0.375
- weight_out: bfloat16 [256, 4], replicated, may hold values from -0.375 to 0.375
Outputs:
- brick_grad: float32 [16384, 4096], P(('group', 'ray'))
Inputs may be any that keep to these rules, and one draw needn't show every extreme that they name: `work_bricks`: slot j of image group g is held by ray index j // 2 of the group, and its brick's owner, the device brick // 32 counted over group then ray, has that same ray index. Among the 2 slots of one device at most 2 name bricks owned in one image group, and on every device exactly 2 do for some group. `tile_slot`: of the 320 tiles of one device, at most 10 name slots held by one device of the group, and on every device some holder is named exactly 10 times.
All inputs are finite; a program needn't handle non-finite values.
Results may differ from a plain program's by a relative error of at most 0.0022.
Values may be sent and summed in bfloat16 or wider, within the bound.
A program may use at most 64 MiB of HBM per device.

v0:
```python
import jax
import jax.numpy as jnp
from jax import lax
from jax.sharding import PartitionSpec as P


def silu_slope(pre_act):
    logistic = jax.nn.sigmoid(pre_act)
    return logistic * (1.0 + pre_act * (1.0 - logistic))


def composite_loss(raw_out, spacing, targets):
    density = jax.nn.softplus(raw_out[:, :, 0])
    shading = jax.nn.sigmoid(raw_out[:, :, 1:4])
    optical = density * spacing
    before_sum = jnp.cumsum(optical, axis=1) - optical
    ray_weight = jnp.exp(-before_sum) * (1.0 - jnp.exp(-optical))
    colour = jnp.sum(ray_weight[:, :, None] * shading, axis=1)
    return 0.5 * jnp.sum((colour - targets.T) ** 2)


def feature_grad(features, spacing, targets, weight_in, weight_mid, weight_out):
    pre_first = jnp.dot(features, weight_in, preferred_element_type=jnp.float32)
    act_first = jax.nn.silu(pre_first).astype(jnp.bfloat16)
    pre_second = jnp.dot(act_first, weight_mid, preferred_element_type=jnp.float32)
    act_second = jax.nn.silu(pre_second).astype(jnp.bfloat16)
    raw_out = jnp.dot(act_second, weight_out, preferred_element_type=jnp.float32)
    ray_count = spacing.shape[0]
    raw_grad = jax.grad(composite_loss)(raw_out.reshape(ray_count, -1, 4), spacing, targets)
    raw_grad = raw_grad.reshape(-1, 4).astype(jnp.bfloat16)
    grad_second = jnp.dot(raw_grad, weight_out.T, preferred_element_type=jnp.float32)
    slope_second = (grad_second * silu_slope(pre_second)).astype(jnp.bfloat16)
    grad_first = jnp.dot(slope_second, weight_mid.T, preferred_element_type=jnp.float32)
    slope_first = (grad_first * silu_slope(pre_first)).astype(jnp.bfloat16)
    return jnp.dot(slope_first, weight_in.T, preferred_element_type=jnp.float32).astype(
        jnp.bfloat16
    )


def earlier_equal(labels):
    order_index = jnp.arange(labels.shape[0])
    matches = (labels[:, None] == labels[None, :]) & (order_index[None, :] < order_index[:, None])
    return jnp.sum(matches.astype(jnp.int32), axis=1)


def per_device(
    bricks, work_bricks, interp, tile_slot, spacing, targets, weight_in, weight_mid, weight_out
):
    own_count = bricks.shape[0]
    row_width = bricks.shape[1]
    held_count = work_bricks.shape[1]
    channels = weight_in.shape[0]
    voxels = row_width // channels
    rays_dev, segments, span = interp.shape
    samples = span // voxels
    tiles_dev = rays_dev * segments
    group_size = lax.axis_size("group")
    ray_size = lax.axis_size("ray")
    per_owner = 1 + (held_count + group_size - 2) // group_size
    entries = work_bricks[0]
    owner_group = entries // own_count // ray_size
    local_id = entries % own_count
    entry_rank = earlier_equal(owner_group)
    requests = (
        jnp.full((group_size, per_owner), -1, jnp.int32).at[owner_group, entry_rank].set(local_id)
    )
    asked = lax.all_to_all(requests, "group", split_axis=0, concat_axis=0, tiled=True)
    wanted = asked >= 0
    picked = jnp.take(bricks, jnp.where(wanted, asked, 0).reshape(-1), axis=0)
    picked = jnp.where(
        wanted[:, :, None],
        picked.reshape(group_size, per_owner, row_width),
        jnp.zeros((), jnp.bfloat16),
    )
    fetched = lax.all_to_all(picked, "group", split_axis=0, concat_axis=0, tiled=True)
    holdings = fetched[owner_group, entry_rank]
    group_set = lax.all_gather(holdings, "ray", axis=0, tiled=True)
    weights_tiles = interp.reshape(tiles_dev, samples, voxels)
    slots = tile_slot.reshape(-1)
    tiles = jnp.take(group_set, slots, axis=0).reshape(tiles_dev, voxels, channels)
    made = jnp.einsum("tiv,tvc->tic", weights_tiles, tiles, preferred_element_type=jnp.float32)
    features = made.astype(jnp.bfloat16).reshape(-1, channels)
    tile_gradients = feature_grad(features, spacing, targets, weight_in, weight_mid, weight_out)
    grads_tiles = tile_gradients.reshape(tiles_dev, samples, channels)
    outer = jnp.einsum(
        "tiv,tic->tvc", weights_tiles, grads_tiles, preferred_element_type=jnp.float32
    )
    group_grad = jax.ops.segment_sum(
        outer.reshape(tiles_dev, row_width), slots, num_segments=held_count * ray_size
    )
    slot_grad = lax.psum_scatter(group_grad, "ray", scatter_dimension=0, tiled=True)
    outgoing = (
        jnp.zeros((group_size, per_owner, row_width), jnp.float32)
        .at[owner_group, entry_rank]
        .set(slot_grad)
    )
    arrived = lax.all_to_all(outgoing, "group", split_axis=0, concat_axis=0, tiled=True).reshape(
        group_size * per_owner, row_width
    )
    destination = jnp.where(wanted, asked, own_count).reshape(-1)
    return jax.ops.segment_sum(arrived, destination, num_segments=own_count + 1)[:own_count]


def solution(mesh):
    in_specs = (
        P(("group", "ray"), None),
        P("group", "ray"),
        P(("group", "ray"), None, None),
        P(("group", "ray"), None),
        P(("group", "ray"), None),
        P(None, ("group", "ray")),
        P(),
        P(),
        P(),
    )
    out_specs = P(("group", "ray"), None)
    return jax.shard_map(
        per_device, mesh=mesh, in_specs=in_specs, out_specs=out_specs, check_vma=False
    )
```

profile of v0, /device:TPU:31, one launch (start us, length us, event | category | flops | bytes accessed | tf_op | source)
XLA Modules:
  0.0 438.0 jit_solution(10257369317479114690)
XLA Ops:
  9.6 16.4 %all_to_all.25 = s32[8,1,2]{2,1,0:T(1,128)S(1)} all-to-all(s32[8,1,2]{2,1,0:T(1,128)S(1)} %copy.55), channel_id=1, replica_groups=mesh['group'=8,'ray'=64] {'group'}, dimensions={0} | all-to-all | bytes 128 | tf_op jit(solution)/shard_map/all_to_all | solution.py:67
  29.0 10.4 %all_to_all.26 = bf16[8,2,4096]{2,1,0:T(2,128)(2,1)S(1)} all-to-all(bf16[8,2,4096]{2,1,0:T(2,128)(2,1)S(1)} %broadcast_select_fusion.2), channel_id=1, replica_groups=mesh['group'=8,'ray'=64] {'group'}, dimensions={0} | all-to-all | bytes 262144 | tf_op jit(solution)/shard_map/all_to_all | solution.py:75
  43.4 77.1 %all-gather.3.cloned.1.call-done = bf16[64,2,4096]{2,1,0:T(2,128)(2,1)} async-done(((bf16[1,2,4096]{2,1,0:T(2,128)(2,1)}), bf16[64,2,4096]{2,1,0:T(2,128)(2,1)}) %all-gather.3.cloned.1.call-update) | async-done | bytes 1048592 | tf_op jit(solution)/shard_map/all_gather | solution.py:77
  121.9 3.9 gather_fusion.2
  125.8 3.3 copy.61
  129.1 2.0 broadcast_select_fusion
  131.1 10.1 %copy.63 = bf16[320,64,64]{2,1,0:T(8,128)(2,1)} copy(bf16[320,64,64]{0,2,1:T(8,128)(2,1)} %broadcast_select_fusion) | data formatting | bytes 5242880 | tf_op jit(solution)/shard_map/jit(_take)/select_n | solution.py:80
  141.2 4.3 fusion.8
  145.5 1.7 fusion.4
  147.3 1.5 copy-done.8
  150.2 1.6 reshape.279
  153.2 1.6 reduce_window_sum.22
  156.6 1.6 fusion.12
  160.2 1.6 reduce_window_sum.23
  162.7 1.5 add_convert_fusion
  164.3 1.6 convert_element_type.36
  165.8 4.0 fusion
  169.8 3.3 convolution_convert_fusion
  174.4 4.9 %convolution_bitcast_fusion = f32[320,64,64]{1,2,0:T(8,128)} fusion(bf16[320,8,64]{2,1,0:T(8,128)(2,1)S(1)} %copy-done.1, bf16[2560,64]{1,0:T(8,128)(2,1)S(1)} %copy.66), kind=kOutput, calls=%fused_computation.11 | convolution fusion | flops 20971520 | bytes 5898240 | tf_op jit(solution)/shard_map/tiv,tic->tvc/dot_general | solution.py:85
  179.3 11.8 %copy.67 = f32[320,64,64]{0,2,1:T(8,128)} copy(f32[320,64,64]{1,2,0:T(8,128)} %convolution_bitcast_fusion) | data formatting | bytes 10485760 | tf_op jit(solution)/shard_map/tiv,tic->tvc/dot_general | solution.py:85
  191.1 6.2 %copy.68 = f32[320,4096]{1,0:T(8,128)} copy(f32[320,4096]{0,1:T(8,128)} %bitcast.97) | data formatting | bytes 10485760 | tf_op jit(solution)/shard_map/reshape | solution.py:89
  197.4 10.6 %scatter_custom_fusion.1 = f32[128,4096]{1,0:T(8,128)} fusion(s32[320]{0:T(512)S(1)} %reshape.313, f32[320,4096]{1,0:T(8,128)} %copy.68, f32[]{:T(128)} %constant.85.clone.1), kind=kCustom, calls=%fused_computation.23 | custom fusion | flops 1310720 | bytes 2097664 | tf_op jit(solution)/shard_map/scatter-add | solution.py:88
  209.9 198.0 %all-reduce.5.cloned.1.call-done = f32[128,4096]{1,0:T(8,128)} async-done(((f32[128,4096]{1,0:T(8,128)}), f32[128,4096]{1,0:T(8,128)}) %all-reduce.5.cloned.1.call-update) | async-done | bytes 2097168
  409.6 19.3 %all_to_all.27 = f32[8,2,4096]{2,1,0:T(2,128)S(1)} all-to-all(f32[8,2,4096]{2,1,0:T(2,128)S(1)} %scatter_fusion.1), channel_id=1, replica_groups=mesh['group'=8,'ray'=64] {'group'}, dimensions={0} | all-to-all | bytes 524288 | tf_op jit(solution)/shard_map/all_to_all | solution.py:97
  (67 shorter events, 25.5 us)
Async XLA Ops:
  6.5 21.2 %copy-start = (bf16[32,4096]{1,0:T(8,128)(2,1)S(1)}, bf16[32,4096]{1,0:T(8,128)(2,1)}, u32[]{:S(2)}) copy-start(bf16[32,4096]{1,0:T(8,128)(2,1)} %param.9) | copy-start | bytes 786436
  6.5 34.2 %copy-start.5 = (s32[64,5]{0,1:T(8,128)S(1)}, s32[64,5]{0,1:T(8,128)}, u32[]{:S(2)}) copy-start(s32[64,5]{0,1:T(8,128)} %param.12) | copy-start | bytes 3844
  6.5 34.6 %copy-start.2 = (bf16[64,5,512]{2,0,1:T(8,128)(2,1)S(1)}, bf16[64,5,512]{2,0,1:T(8,128)(2,1)}, u32[]{:S(2)}) copy-start(bf16[64,5,512]{2,0,1:T(8,128)(2,1)} %param.11) | copy-start | bytes 983044
  6.5 113.9 %all-gather.3.cloned.1.call-start = ((), (), s32[]{:S(2)}) async-start(), calls=%async_computation.3 | async-start | bytes 1064960 | tf_op jit(solution)/shard_map/all_gather | solution.py:77
  8.8 33.8 %copy-start.4 = (f32[64,40]{0,1:T(8,128)S(1)}, f32[64,40]{0,1:T(8,128)}, u32[]{:S(2)}) copy-start(f32[64,40]{0,1:T(8,128)} %param.13) | copy-start | bytes 30724
  40.7 367.2 %all-reduce.5.cloned.1.call-start = ((), (), s32[]{:S(2)}) async-start(), calls=%async_computation.4 | async-start | bytes 4194304
  131.1 10.1 %copy-start.1 = (bf16[320,8,64]{2,1,0:T(8,128)(2,1)S(1)}, bf16[320,8,64]{2,1,0:T(8,128)(2,1)}, u32[]{:S(2)}) copy-start(bf16[320,8,64]{2,1,0:T(8,128)(2,1)} %reshape.277) | copy-start | bytes 983044
  145.5 3.3 copy-start.7
  147.3 1.5 copy-start.8
  148.8 7.8 %copy-start.6 = (f32[3,64]{1,0:T(4,128)S(1)}, f32[3,64]{1,0:T(4,128)}, u32[]{:S(2)}) copy-start(f32[3,64]{1,0:T(4,128)} %param.14) | copy-start | bytes 2308
  158.2 0.6 copy-start.3
Sparse Core Ops, SparseCore 0:
  40.8 79.5 all-gather.2
  208.1 199.7 all-reduce.4
where the time goes:
time: 439 us; the launch traced here: 438 us
  waiting for transfers between devices  275 us (63%)
  local copies, waits for them, and re-layouts  53.5 us (12%)
  blocking collectives  46.1 us (11%)
  other arithmetic  29.4 us (7%)
  matrix products  19.6 us (4%)
  between operations  14.3 us (3%)
    unnamed x3, waiting for transfers between devices  198 us
    all_gather x1, waiting for transfers between devices, per_device(): group_set = lax.all_gather(holdings, 'ray', axis=0, tiled=True)  77.1 us
    all_to_all x1, blocking collectives, per_device(): lax.all_to_all(outgoing, 'group', split_axis=0, concat_axis=0, tiled=True)  19.3 us
    all_to_all x1, blocking collectives, per_device(): lax.all_to_all(requests, 'group', split_axis=0, concat_axis=0, tiled=True)  16.4 us
    dot_general x1, local copies, waits for them, and re-layouts, per_device(): jnp.einsum('tiv,tic->tvc', weights_tiles, grads_tiles, preferred_element_...  11.8 us
    scatter-add x1, other arithmetic, per_device(): jax.ops.segment_sum(outer.reshape(tiles_dev, row_width), slots, num_segme...  10.6 us
    all_to_all x1, blocking collectives, per_device(): lax.all_to_all(picked, 'group', split_axis=0, concat_axis=0, tiled=True)  10.4 us
    select_n x1, local copies, waits for them, and re-layouts, per_device(): jnp.take(group_set, slots, axis=0).reshape(tiles_dev, voxels, channels)  10.1 us
  transfers between devices with their start and end apart: 2, of which 2 were waited for; matrix products, arithmetic and copies ran while one was open for 1% of the time, Pallas kernels for 0%

commit v1 on v0

--- a/solution.py
+++ b/solution.py
@@ -2,6 +2,11 @@
 import jax.numpy as jnp
 from jax import lax
 from jax.sharding import PartitionSpec as P
+
+
+def swapped_in(x, axis, dim):
+    sent = jnp.stack([x] * lax.axis_size(axis))
+    return jnp.concatenate(lax.all_to_all(sent, axis, 0, 0), axis=dim)
 
 
 def silu_slope(pre_act):
@@ -74,7 +79,7 @@
     )
     fetched = lax.all_to_all(picked, "group", split_axis=0, concat_axis=0, tiled=True)
     holdings = fetched[owner_group, entry_rank]
-    group_set = lax.all_gather(holdings, "ray", axis=0, tiled=True)
+    group_set = swapped_in(holdings, "ray", 0)
     weights_tiles = interp.reshape(tiles_dev, samples, voxels)
     slots = tile_slot.reshape(-1)
     tiles = jnp.take(group_set, slots, axis=0).reshape(tiles_dev, voxels, channels)

time: 439 us -> 393 us (0.90)
  waiting for transfers between devices: 275 us -> 215 us
  starting transfers between devices: 0.04 us -> 13.2 us
    all_gather x1 -> x0, waiting for transfers between devices: 77.1 us -> none  [per_device(): group_set = lax.all_gather(holdings, 'ray', axis=0, tiled=True)]
    all_to_all x0 -> x1, waiting for transfers between devices: none -> 23.1 us  [swapped_in(): return jnp.concatenate(lax.all_to_all(sent, axis, 0, 0), axis=dim)]
    all_to_all x0 -> x1, starting transfers between devices: none -> 13.1 us  [swapped_in(): return jnp.concatenate(lax.all_to_all(sent, axis, 0, 0), axis=dim)]
    unnamed x3 -> x2, waiting for transfers between devices: 198 us -> 192 us
where the time goes in v1:
time: 393 us; the launch traced here: 392 us
  waiting for transfers between devices  215 us (55%)
  local copies, waits for them, and re-layouts  53.9 us (14%)
  blocking collectives  46.1 us (12%)
  other arithmetic  29.4 us (7%)
  matrix products  19.7 us (5%)
  between operations  14.3 us (4%)
  starting transfers between devices  13.2 us (3%)
    unnamed x2, waiting for transfers between devices  192 us
    all_to_all x1, waiting for transfers between devices, swapped_in(): return jnp.concatenate(lax.all_to_all(sent, axis, 0, 0), axis=dim)  23.1 us
    all_to_all x1, blocking collectives, per_device(): lax.all_to_all(outgoing, 'group', split_axis=0, concat_axis=0, tiled=True)  19.3 us
    all_to_all x1, blocking collectives, per_device(): lax.all_to_all(requests, 'group', split_axis=0, concat_axis=0, tiled=True)  16.4 us
    all_to_all x1, starting transfers between devices, swapped_in(): return jnp.concatenate(lax.all_to_all(sent, axis, 0, 0), axis=dim)  13.1 us
    dot_general x1, local copies, waits for them, and re-layouts, per_device(): jnp.einsum('tiv,tic->tvc', weights_tiles, grads_tiles, preferred_element_...  11.8 us
    scatter-add x1, other arithmetic, per_device(): jax.ops.segment_sum(outer.reshape(tiles_dev, row_width), slots, num_segme...  10.6 us
    all_to_all x1, blocking collectives, per_device(): lax.all_to_all(picked, 'group', split_axis=0, concat_axis=0, tiled=True)  10.4 us
  transfers between devices with their start and end apart: 2, of which 2 were waited for; matrix products, arithmetic and copies ran while one was open for 1% of the time, Pallas kernels for 0%

profile of v1, /device:TPU:31, one launch (start us, length us, event | category | flops | bytes accessed | tf_op | source)
XLA Modules:
  0.0 391.7 jit_solution(10210058238951387267)
XLA Ops:
  9.5 16.4 %all_to_all.30 = s32[8,1,2]{2,1,0:T(1,128)S(1)} all-to-all(s32[8,1,2]{2,1,0:T(1,128)S(1)} %copy.55), channel_id=1, replica_groups=mesh['group'=8,'ray'=64] {'group'}, dimensions={0} | all-to-all | bytes 128 | tf_op jit(solution)/shard_map/all_to_all | solution.py:72
  29.0 10.4 %all_to_all.31 = bf16[8,2,4096]{2,1,0:T(2,128)(2,1)S(1)} all-to-all(bf16[8,2,4096]{2,1,0:T(2,128)(2,1)S(1)} %broadcast_select_fusion.2), channel_id=1, replica_groups=mesh['group'=8,'ray'=64] {'group'}, dimensions={0} | all-to-all | bytes 262144 | tf_op jit(solution)/shard_map/all_to_all | solution.py:80
  40.1 2.0 stack.2
  42.1 13.1 %all-to-all-start.2 = ((bf16[64,2,4096]{2,1,0:T(2,128)(2,1)}), bf16[64,2,4096]{2,1,0:T(2,128)(2,1)S(1)}, u32[]{:S(2)}, u32[]{:S(2)}) async-start(bf16[64,2,4096]{2,1,0:T(2,128)(2,1)} %stack.2), calls=%async_computation.2 | async-start | bytes 2097152 | tf_op jit(solution)/shard_map/all_to_all | solution.py:9
  57.9 23.1 %all-to-all-done.2 = bf16[64,2,4096]{2,1,0:T(2,128)(2,1)S(1)} async-done(((bf16[64,2,4096]{2,1,0:T(2,128)(2,1)}), bf16[64,2,4096]{2,1,0:T(2,128)(2,1)S(1)}, u32[]{:S(2)}, u32[]{:S(2)}) %all-to-all-start.2) | async-done | bytes 1048608 | tf_op jit(solution)/shard_map/all_to_all | solution.py:9
  81.4 3.9 gather_fusion.2
  85.3 3.3 copy.61
  88.6 2.0 broadcast_select_fusion
  90.6 10.1 %copy.63 = bf16[320,64,64]{2,1,0:T(8,128)(2,1)} copy(bf16[320,64,64]{0,2,1:T(8,128)(2,1)} %broadcast_select_fusion) | data formatting | bytes 5242880 | tf_op jit(solution)/shard_map/jit(_take)/select_n | solution.py:85
  100.7 4.3 %fusion.8 = f32[2560,256]{1,0:T(8,128)S(1)} fusion(bf16[64,256]{1,0:T(8,128)(2,1)} %param.15, bf16[320,64,64]{2,1,0:T(8,128)(2,1)} %copy.63, bf16[320,8,64]{2,1,0:T(8,128)(2,1)S(1)} %copy-done.1), kind=kOutput, calls=%fused_computation.25 | convolution fusion | flops 105021440 | bytes 5603328 | tf_op jit(solution)/shard_map/dot_general | solution.py:28
  105.1 1.7 fusion.4
  109.7 1.6 reshape.285
  112.7 1.6 reduce_window_sum.22
  116.1 1.6 fusion.12
  119.7 1.6 reduce_window_sum.23
  123.8 1.6 convert_element_type.36
  125.4 4.0 %fusion = bf16[2560,256]{1,0:T(8,128)(2,1)} fusion(bf16[2560,4]{0,1:T(4,128)(2,1)} %convert_element_type.36, bf16[256,4]{0,1:T(4,128)(2,1)S(1)} %copy-done.7, f32[2560,256]{1,0:T(8,128)} %copy-done.8), kind=kOutput, calls=%fused_computation.9 | convolution fusion | flops 11141120 | bytes 3954688 | tf_op jit(solution)/shard_map/dot_general | solution.py:36
  129.3 3.3 convolution_convert_fusion
  134.0 4.9 %convolution_bitcast_fusion = f32[320,64,64]{1,2,0:T(8,128)} fusion(bf16[320,8,64]{2,1,0:T(8,128)(2,1)S(1)} %copy-done.1, bf16[2560,64]{1,0:T(8,128)(2,1)S(1)} %copy.66), kind=kOutput, calls=%fused_computation.11 | convolution fusion | flops 20971520 | bytes 5898240 | tf_op jit(solution)/shard_map/tiv,tic->tvc/dot_general | solution.py:90
  138.9 11.8 %copy.67 = f32[320,64,64]{0,2,1:T(8,128)} copy(f32[320,64,64]{1,2,0:T(8,128)} %convolution_bitcast_fusion) | data formatting | bytes 10485760 | tf_op jit(solution)/shard_map/tiv,tic->tvc/dot_general | solution.py:90
  150.7 6.2 %copy.68 = f32[320,4096]{1,0:T(8,128)} copy(f32[320,4096]{0,1:T(8,128)} %bitcast.96) | data formatting | bytes 10485760 | tf_op jit(solution)/shard_map/reshape | solution.py:94
  156.9 10.6 %scatter_custom_fusion.1 = f32[128,4096]{1,0:T(8,128)} fusion(s32[320]{0:T(512)S(1)} %reshape.319, f32[320,4096]{1,0:T(8,128)} %copy.68, f32[]{:T(128)} %constant.85.clone.1), kind=kCustom, calls=%fused_computation.23 | custom fusion | flops 1310720 | bytes 2097664 | tf_op jit(solution)/shard_map/scatter-add | solution.py:93
  169.4 192.1 %all-reduce.5.cloned.1.call-done = f32[128,4096]{1,0:T(8,128)} async-done(((f32[128,4096]{1,0:T(8,128)}), f32[128,4096]{1,0:T(8,128)}) %all-reduce.5.cloned.1.call-update) | async-done | bytes 2097168
  363.3 19.3 %all_to_all.32 = f32[8,2,4096]{2,1,0:T(2,128)S(1)} all-to-all(f32[8,2,4096]{2,1,0:T(2,128)S(1)} %scatter_fusion.1), channel_id=1, replica_groups=mesh['group'=8,'ray'=64] {'group'}, dimensions={0} | all-to-all | bytes 524288 | tf_op jit(solution)/shard_map/all_to_all | solution.py:102
  (67 shorter events, 26.8 us)
Async XLA Ops:
  6.5 21.2 %copy-start = (bf16[32,4096]{1,0:T(8,128)(2,1)S(1)}, bf16[32,4096]{1,0:T(8,128)(2,1)}, u32[]{:S(2)}) copy-start(bf16[32,4096]{1,0:T(8,128)(2,1)} %param.9) | copy-start | bytes 786436
  27.7 27.5 %copy-start.5 = (s32[64,5]{0,1:T(8,128)S(1)}, s32[64,5]{0,1:T(8,128)}, u32[]{:S(2)}) copy-start(s32[64,5]{0,1:T(8,128)} %param.12) | copy-start | bytes 3844
  27.7 27.9 %copy-start.2 = (bf16[64,5,512]{2,0,1:T(8,128)(2,1)S(1)}, bf16[64,5,512]{2,0,1:T(8,128)(2,1)}, u32[]{:S(2)}) copy-start(bf16[64,5,512]{2,0,1:T(8,128)(2,1)} %param.11) | copy-start | bytes 983044
  40.0 17.1 %copy-start.4 = (f32[64,40]{0,1:T(8,128)S(1)}, f32[64,40]{0,1:T(8,128)}, u32[]{:S(2)}) copy-start(f32[64,40]{0,1:T(8,128)} %param.13) | copy-start | bytes 30724
  42.1 39.0 %all-to-all-start.2 = ((bf16[64,2,4096]{2,1,0:T(2,128)(2,1)}), bf16[64,2,4096]{2,1,0:T(2,128)(2,1)S(1)}, u32[]{:S(2)}, u32[]{:S(2)}) async-start(bf16[64,2,4096]{2,1,0:T(2,128)(2,1)} %stack.2), calls=%async_computation.2 | async-start | bytes 2097152 | tf_op jit(solution)/shard_map/all_to_all | solution.py:9
  55.2 306.4 %all-reduce.5.cloned.1.call-start = ((), (), s32[]{:S(2)}) async-start(), calls=%async_computation.4 | async-start | bytes 4194304
  90.6 10.1 %copy-start.1 = (bf16[320,8,64]{2,1,0:T(8,128)(2,1)S(1)}, bf16[320,8,64]{2,1,0:T(8,128)(2,1)}, u32[]{:S(2)}) copy-start(bf16[320,8,64]{2,1,0:T(8,128)(2,1)} %reshape.283) | copy-start | bytes 983044
  105.0 3.3 copy-start.7
  106.8 1.5 copy-start.8
  108.3 7.8 %copy-start.6 = (f32[3,64]{1,0:T(4,128)S(1)}, f32[3,64]{1,0:T(4,128)}, u32[]{:S(2)}) copy-start(f32[3,64]{1,0:T(4,128)} %param.14) | copy-start | bytes 2308
  117.7 0.6 copy-start.3
Sparse Core Ops, SparseCore 0:
  167.6 193.8 all-reduce.4
